TPU v7x, 32 devices: a whole 2x2x4 slice. The times are simulated.
32 devices in a mesh: beam: 4 (over z), pulse: 4 (over x, core), range: 2 (over y).
Axes of the slice: x: 2, y: 2, z: 4, core: 2. Of those that a mesh axis runs over, the one named last changes fastest.
Arguments:
- signal: bfloat16 [8, 32, 2, 1024], P('beam', 'pulse', None, 'range'), may hold values from -40 to 40, as said below
- replica: bfloat16 [2, 2048], P(None, ('beam', 'pulse')), may hold values from -0.09375 to 0.09375
- guard_cells: int32 [8], P('beam'), may hold values from 1 to 8, as said below
- train_cells: int32 [8], P('beam'), may hold values from 64 to 96, as said below
- scale_index: int32 [8], P('beam'), may hold values from 0 to 15
- offsets: int32 [8], P('beam'), may hold values from 0 to 127, as said below
Outputs:
- compressed: bfloat16 [8, 32, 2, 1024], P('beam', 'pulse', None, 'range')
- test_ratio: float32 [8, 32, 1024], P('beam', 'pulse', 'range')
Inputs may be any that keep to these rules, and one draw needn't show every extreme that they name: `signal`: values stay within the range, with cell-to-cell varying levels. `guard_cells`: some beam has exactly 8 guard cells. `train_cells`: the beam with 8 guard cells has 96 training cells. `offsets`: some beam has the offset 128 - 1.
All inputs are finite; a program needn't handle non-finite values.
Results may differ from a plain program's by a relative error of at most 0.001.
Values may be sent and summed in bfloat16 or wider, within the bound.
A program may use at most 64 MiB of HBM per device.

v0:
```python
import jax
import jax.numpy as jnp
from jax import lax
from jax.sharding import PartitionSpec as P

TILE = 128
OFF_MAX = 128
GUARD_MAX = 8
TRAIN_MAX = 96


EPSILON = 1e-06


def passed_along(array, axis, by):
    devices = lax.axis_size(axis)
    pairs = [(i, i + by) for i in range(devices) if 0 <= i + by < devices]
    return lax.ppermute(array, axis, pairs)


def padded_2(cells, sides, width):
    for axis, dim in sides:
        count = lax.axis_size(axis)
        ends = count - 1
        head = lax.slice_in_dim(cells, 0, width, axis=dim)
        tail = lax.slice_in_dim(cells, cells.shape[dim] - width, cells.shape[dim], axis=dim)
        cells = jnp.concatenate(
            [
                lax.ppermute(tail, axis, [(i, (i + 1) % count) for i in range(ends)]),
                cells,
                lax.ppermute(head, axis, [((i + 1) % count, i) for i in range(ends)]),
            ],
            axis=dim,
        )
    return cells


def panels(whole):
    width = TILE + whole.shape[1]

    def skewed(values):
        padded = jnp.concatenate([values, jnp.zeros((TILE + 1,), values.dtype)])
        flat = jnp.tile(padded, TILE)[: TILE * width]
        return flat.reshape(TILE, width)

    return (skewed(whole[0]), skewed(whole[1]))


def compress(extended, offsets, panel_real, panel_imag, tiles):
    beams, pulses = (extended.shape[0], extended.shape[1])
    width = panel_real.shape[1]
    span = tiles * TILE + width - TILE

    def align(block, start):
        return lax.dynamic_slice_in_dim(block, start, span, 2)

    aligned = jax.vmap(align)(extended, offsets)
    rows = beams * pulses
    group = max(1, min(tiles, 256 // rows))
    while tiles % group:
        group = group - 1
    blocks = tiles // group
    dims = (((1,), (1,)), ((), ()))

    def block_fn(index):
        first = index * (group * TILE)
        windows = jnp.stack(
            [
                lax.dynamic_slice_in_dim(aligned, first + step * TILE, width, 3)
                for step in range(group)
            ]
        )
        real_part = windows[:, :, :, 0, :].reshape(group * rows, width)
        imag_part = windows[:, :, :, 1, :].reshape(group * rows, width)
        out_real = lax.dot_general(
            real_part, panel_real, dims, preferred_element_type=jnp.float32
        ) + lax.dot_general(imag_part, panel_imag, dims, preferred_element_type=jnp.float32)
        out_imag = lax.dot_general(
            imag_part, panel_real, dims, preferred_element_type=jnp.float32
        ) - lax.dot_general(real_part, panel_imag, dims, preferred_element_type=jnp.float32)
        return jnp.stack([out_real, out_imag], axis=1).reshape(group, beams, pulses, 2, TILE)

    outputs = lax.map(block_fn, jnp.arange(blocks, dtype=jnp.int32))
    outputs = outputs.reshape(tiles, beams, pulses, 2, TILE)
    return jnp.transpose(outputs, (1, 2, 3, 0, 4)).reshape(beams, pulses, 2, tiles * TILE)


def cell_power(compressed):
    real_part = compressed[:, :, 0].astype(jnp.float32)
    imag_part = compressed[:, :, 1].astype(jnp.float32)
    return real_part * real_part + imag_part * imag_part


def detect(padded, guard_cells, train_cells, scale_index, first_gate, total_gates):
    margin = GUARD_MAX + TRAIN_MAX
    beams, pulses = (padded.shape[0], padded.shape[1])
    length = padded.shape[2] - 2 * margin
    running = jnp.cumsum(padded, axis=2)
    prefix = jnp.concatenate([jnp.zeros((beams, pulses, 1), jnp.float32), running], axis=2)
    local = jnp.arange(length, dtype=jnp.int32)[None, :]
    guard = guard_cells[:, None]
    train = train_cells[:, None]

    def window(block, start):
        return lax.dynamic_slice_in_dim(block, start, length, 1)

    def pick(starts):
        return jax.vmap(window)(prefix, starts)

    lag = pick(margin - guard_cells) - pick(margin - guard_cells - train_cells)
    lead = pick(margin + guard_cells + train_cells + 1) - pick(margin + guard_cells + 1)
    position = first_gate + local
    count = jnp.clip(position - guard, 0, train) + jnp.clip(
        total_gates - 1 - position - guard, 0, train
    )
    noise = (lag + lead) / count.astype(jnp.float32)[:, None, :]
    factor = jnp.exp2(scale_index.astype(jnp.float32) / 8.0)
    power = padded[:, :, margin : margin + length]
    return power / (factor[:, None, None] * (noise + EPSILON))


def body(signal, replica, guard_cells, train_cells, scale_index, offsets):
    whole = lax.all_gather(replica, ("beam", "pulse"), axis=1, tiled=True)
    panel_real, panel_imag = panels(whole)
    gate_count = signal.shape[3]
    margin = GUARD_MAX + TRAIN_MAX
    needed = whole.shape[1] + OFF_MAX
    limit = min(-(-needed // gate_count), lax.axis_size("range") - 1)
    pieces = [signal]
    for step in range(1, limit + 1):
        keep = min(gate_count, needed - (step - 1) * gate_count)
        pieces.append(passed_along(signal[:, :, :, :keep], "range", -step))
    extended = jnp.concatenate(pieces, axis=3)
    extra = gate_count + needed - extended.shape[3]
    extended = jnp.pad(extended, ((0, 0), (0, 0), (0, 0), (0, extra)))
    compressed = compress(extended, offsets, panel_real, panel_imag, gate_count // TILE).astype(
        jnp.bfloat16
    )
    power = cell_power(compressed)
    padded = padded_2(power, (("range", 2),), margin)
    first_gate = lax.axis_index("range") * gate_count
    total_gates = gate_count * lax.axis_size("range")
    test_ratio = detect(padded, guard_cells, train_cells, scale_index, first_gate, total_gates)
    return (compressed, test_ratio)


def solution(mesh):
    placed = (
        P("beam", "pulse", None, "range"),
        P(None, ("beam", "pulse")),
        P("beam"),
        P("beam"),
        P("beam"),
        P("beam"),
    )
    return jax.shard_map(
        body,
        mesh=mesh,
        in_specs=placed,
        out_specs=(P("beam", "pulse", None, "range"), P("beam", "pulse", "range")),
        check_vma=False,
    )
```

profile of v0, /device:TPU:0, one launch (start us, length us, event | category | flops | bytes accessed | tf_op | source)
XLA Modules:
  0.0 62.5 jit_solution(7068981721563648878)
XLA Ops:
  0.6 1.3 %collective-permute-start = (bf16[2,8,2,512]{3,2,1,0:T(2,128)(2,1)}, bf16[2,8,2,512]{3,2,1,0:T(2,128)(2,1)S(1)}, u32[]{:S(2)}, u32[]{:S(2)}) collective-permute-start(bf16[2,8,2,512]{3,2,1,0:T(2,128)(2,1)} %param.6), channel_id=1, source_target_pairs={{1,0},{3,2},{5,4},{7,6},{9,8},{11,10},{13,12},{15,14},{17,16},{19,... | collective-permute-start | bytes 98312 | tf_op jit(solution)/shard_map/ppermute | solution.py:18
  1.9 0.6 %copy-done.4 = s32[2]{0:T(128)S(1)} copy-done((s32[2]{0:T(128)S(1)}, s32[2]{0:T(128)}, u32[]{:S(2)}) %copy-start.4) | copy-done | bytes 32
  2.6 0.6 %copy-done.3 = bf16[2,128]{1,0:T(2,128)(2,1)S(1)} copy-done((bf16[2,128]{1,0:T(2,128)(2,1)S(1)}, bf16[2,128]{1,0:T(2,128)(2,1)}, u32[]{:S(2)}) %copy-start.3) | copy-done | bytes 536
  3.2 23.1 %all_gather.3 = bf16[2,2048]{1,0:T(2,128)(2,1)S(1)} all-gather(bf16[2,128]{1,0:T(2,128)(2,1)S(1)} %copy-done.3), channel_id=1, replica_groups=mesh['beam'=4,'pulse'=4,'range'=2] {'beam','pulse'}, dimensions={1}, use_global_device_ids=true | all-gather | bytes 8704 | tf_op jit(solution)/shard_map/all_gather | solution.py:123
  26.4 0.6 copy-done.1
  27.3 0.7 %tile.9 = bf16[278656]{0:T(1024)(128)(2,1)S(1)} reshape(bf16[128,2177]{1,0:T(8,128)(2,1)S(1)} %tile.8) | data formatting | bytes 1114624 | tf_op jit(solution)/shard_map/tile | solution.py:43
  28.0 0.6 reshape.119
  28.7 0.7 %tile.21 = bf16[278656]{0:T(1024)(128)(2,1)S(1)} reshape(bf16[128,2177]{1,0:T(8,128)(2,1)S(1)} %tile.20) | data formatting | bytes 1114624 | tf_op jit(solution)/shard_map/tile | solution.py:43
  29.5 0.6 reshape.120
  30.4 4.0 %while.1 = (s32[]{:T(128)}, bf16[2,8,2,2688]{3,2,1,0:T(2,128)(2,1)S(1)}, s32[2,4]{1,0:T(2,128)S(1)}, bf16[2,8,2,2560]{3,1,0,2:T(8,128)(2,1)S(1)}, s32[]{:T(128)}) while((s32[]{:T(128)}, bf16[2,8,2,2688]{3,2,1,0:T(2,128)(2,1)S(1)}, s32[2,4]{1,0:T(2,128)S(1)}, bf16[2,8,2,2560]{3,1,0,2:T(8,128)(2,1)S(1)}, s32[]{:T(128)}) %tuple.43), condition=%wide.while_cond, body=%wide.while_body.sunk | while | flops 2 | bytes 327813 | solution.py:55
  30.4 0.6 fusion.34
  31.0 1.4 %constant_dynamic-slice_fusion.5 = bf16[1,8,2,2560]{3,2,1,0:T(2,128)(2,1)S(1)} fusion(bf16[2,8,2,2688]{3,2,1,0:T(2,128)(2,1)S(1)} %get-tuple-element.115, s32[]{:T(128)} %bitcast.68, s32[]{:T(128)} %bitcast.69), kind=kLoop, calls=%fused_computation.6.clone.1 | loop fusion | bytes 163848 | tf_op jit(solution)/shard_map/vmap()/gather
  32.4 0.6 fusion.34
  33.0 1.4 %constant_dynamic-slice_fusion.5 = bf16[1,8,2,2560]{3,2,1,0:T(2,128)(2,1)S(1)} fusion(bf16[2,8,2,2688]{3,2,1,0:T(2,128)(2,1)S(1)} %get-tuple-element.115, s32[]{:T(128)} %bitcast.68, s32[]{:T(128)} %bitcast.69), kind=kLoop, calls=%fused_computation.6.clone.1 | loop fusion | bytes 163848 | tf_op jit(solution)/shard_map/vmap()/gather
  36.0 4.7 %collective-permute-start.1 = (f32[2,8,104]{2,1,0:T(8,128)S(1)}, f32[2,8,104]{2,1,0:T(8,128)S(1)}, u32[]{:S(2)}, u32[]{:S(2)}) collective-permute-start(f32[2,8,104]{2,1,0:T(8,128)S(1)} %get-tuple-element.67), channel_id=1, source_target_pairs={{0,1},{2,3},{4,5},{6,7},{8,9},{10,11},{12,13},{14,15},{16,17},{18,... | collective-permute-start | bytes 19976 | tf_op jit(solution)/shard_map/ppermute | solution.py:29
  40.7 1.5 %collective-permute-start.2 = (f32[2,8,104]{2,1,0:T(8,128)S(1)}, f32[2,8,104]{2,1,0:T(8,128)S(1)}, u32[]{:S(2)}, u32[]{:S(2)}) collective-permute-start(f32[2,8,104]{2,1,0:T(8,128)S(1)} %get-tuple-element.68), channel_id=1, source_target_pairs={{1,0},{3,2},{5,4},{7,6},{9,8},{11,10},{13,12},{15,14},{17,16},{19,... | collective-permute-start | bytes 19976 | tf_op jit(solution)/shard_map/ppermute | solution.py:31
  42.2 0.6 %copy.55 = bf16[2,8,2,512]{3,2,1,0:T(2,128)(2,1)} copy(bf16[2,8,2,512]{3,1,2,0:T(8,128)(2,1)S(1)} %copy_bitcast_fusion) | data formatting | bytes 65536
  42.8 3.4 %collective-permute-done.2 = f32[2,8,104]{2,1,0:T(8,128)S(1)} collective-permute-done((f32[2,8,104]{2,1,0:T(8,128)S(1)}, f32[2,8,104]{2,1,0:T(8,128)S(1)}, u32[]{:S(2)}, u32[]{:S(2)}) %collective-permute-start.2) | collective-permute-done | bytes 6688 | tf_op jit(solution)/shard_map/ppermute | solution.py:31
  46.3 3.4 %reduce-window.6 = f32[2,8,6,128]{3,1,2,0:T(8,128)S(1)} reduce-window(f32[2,8,6,128]{3,1,2,0:T(8,128)S(1)} %fusion.5, f32[]{:T(128)} %constant.72.clone.1), window={size=1x1x1x128 pad=0_0x0_0x0_0x127_0}, to_apply=%region_0.1 | reduce-window | flops 1560576 | bytes 98308 | tf_op jit(solution)/shard_map/reduce-window
  50.6 2.6 %gather_fusion.3 = f32[2,8,512]{1,0,2:T(2,128)S(1)} fusion(f32[2,8,721]{1,0,2:T(2,128)S(1)} %concatenate.37, s32[2]{0:T(128)S(1)} %get-tuple-element.72), kind=kCustom, calls=%fused_computation.3 | custom fusion | bytes 65560 | tf_op jit(solution)/shard_map/vmap()/gather | solution.py:105
  53.4 2.6 %gather_fusion.2 = f32[2,8,512]{1,0,2:T(2,128)S(1)} fusion(f32[2,8,721]{1,0,2:T(2,128)S(1)} %concatenate.37, s32[2]{0:T(128)S(1)} %get-tuple-element.70), kind=kCustom, calls=%fused_computation.2 | custom fusion | bytes 65560 | tf_op jit(solution)/shard_map/vmap()/gather | solution.py:105
  56.2 2.6 %gather_fusion.1 = f32[2,8,512]{1,0,2:T(2,128)S(1)} fusion(f32[2,8,721]{1,0,2:T(2,128)S(1)} %concatenate.37, s32[2]{0:T(128)S(1)} %get-tuple-element.69), kind=kCustom, calls=%fused_computation.1 | custom fusion | bytes 65560 | tf_op jit(solution)/shard_map/vmap()/gather | solution.py:105
  59.0 2.6 %gather_fusion = f32[2,8,512]{1,0,2:T(2,128)S(1)} fusion(f32[2,8,721]{1,0,2:T(2,128)S(1)} %concatenate.37, s32[2]{0:T(128)S(1)} %get-tuple-element.71), kind=kCustom, calls=%fused_computation | custom fusion | bytes 65560 | tf_op jit(solution)/shard_map/vmap()/gather | solution.py:105
  61.8 0.7 %multiply_divide_fusion = f32[2,8,512]{2,1,0:T(8,128)} fusion(f32[2,8,512]{2,1,0:T(8,128)S(1)} %copy.53, f32[2,8,512]{2,1,0:T(8,128)S(1)} %copy.54, f32[2,8,512]{2,1,0:T(8,128)S(1)} %copy.51, f32[2,8,512]{2,1,0:T(8,128)S(1)} %copy.52, f32[2,512]{1,0:T(2,128)S(1)} %add_convert_fusion, f32[2]{0:T(128)S(1)} %multiply_exponential_fusion, ...), kind=kLoop, calls=%fused_computation.27 | loop fusion | flops 98304 | bytes 200712 | tf_op jit(solution)/shard_map/div | solution.py:119
  (55 shorter events, 4.0 us)
Async XLA Ops:
  0.6 29.5 %collective-permute-start = (bf16[2,8,2,512]{3,2,1,0:T(2,128)(2,1)}, bf16[2,8,2,512]{3,2,1,0:T(2,128)(2,1)S(1)}, u32[]{:S(2)}, u32[]{:S(2)}) collective-permute-start(bf16[2,8,2,512]{3,2,1,0:T(2,128)(2,1)} %param.6), channel_id=1, source_target_pairs={{1,0},{3,2},{5,4},{7,6},{9,8},{11,10},{13,12},{15,14},{17,16},{19,... | collective-permute-start | bytes 98312 | tf_op jit(solution)/shard_map/ppermute | solution.py:18
  1.9 0.7 %copy-start.4 = (s32[2]{0:T(128)S(1)}, s32[2]{0:T(128)}, u32[]{:S(2)}) copy-start(s32[2]{0:T(128)} %param.11) | copy-start | bytes 28
  2.6 0.7 %copy-start.3 = (bf16[2,128]{1,0:T(2,128)(2,1)S(1)}, bf16[2,128]{1,0:T(2,128)(2,1)}, u32[]{:S(2)}) copy-start(bf16[2,128]{1,0:T(2,128)(2,1)} %param.7) | copy-start | bytes 1540
  26.3 0.7 %copy-start.1 = (s32[2]{0:T(128)S(1)}, s32[2]{0:T(128)}, u32[]{:S(2)}) copy-start(s32[2]{0:T(128)} %param.9) | copy-start | bytes 28
  26.3 0.7 %copy-start.2 = (s32[2]{0:T(128)S(1)}, s32[2]{0:T(128)}, u32[]{:S(2)}) copy-start(s32[2]{0:T(128)} %param.8) | copy-start | bytes 28
  29.5 0.8 %copy-start = (bf16[2,8,2,512]{3,2,1,0:T(2,128)(2,1)S(1)}, bf16[2,8,2,512]{3,2,1,0:T(2,128)(2,1)}, u32[]{:S(2)}) copy-start(bf16[2,8,2,512]{3,2,1,0:T(2,128)(2,1)} %param.6) | copy-start | bytes 98308
  36.0 6.2 %copy-start.5 = (s32[2]{0:T(128)S(1)}, s32[2]{0:T(128)}, u32[]{:S(2)}) copy-start(s32[2]{0:T(128)} %param.10) | copy-start | bytes 28
  36.0 6.8 %collective-permute-start.1 = (f32[2,8,104]{2,1,0:T(8,128)S(1)}, f32[2,8,104]{2,1,0:T(8,128)S(1)}, u32[]{:S(2)}, u32[]{:S(2)}) collective-permute-start(f32[2,8,104]{2,1,0:T(8,128)S(1)} %get-tuple-element.67), channel_id=1, source_target_pairs={{0,1},{2,3},{4,5},{6,7},{8,9},{10,11},{12,13},{14,15},{16,17},{18,... | collective-permute-start | bytes 19976 | tf_op jit(solution)/shard_map/ppermute | solution.py:29
  40.7 5.5 %collective-permute-start.2 = (f32[2,8,104]{2,1,0:T(8,128)S(1)}, f32[2,8,104]{2,1,0:T(8,128)S(1)}, u32[]{:S(2)}, u32[]{:S(2)}) collective-permute-start(f32[2,8,104]{2,1,0:T(8,128)S(1)} %get-tuple-element.68), channel_id=1, source_target_pairs={{1,0},{3,2},{5,4},{7,6},{9,8},{11,10},{13,12},{15,14},{17,16},{19,... | collective-permute-start | bytes 19976 | tf_op jit(solution)/shard_map/ppermute | solution.py:31
where the time goes:
time: 62.8 us; the launch traced here: 62.5 us
  blocking collectives  23.1 us (37%)
  local copies, waits for them, and re-layouts  21.7 us (35%)
  starting transfers between devices  7.43 us (12%)
  other arithmetic  4.6 us (7%)
  waiting for transfers between devices  3.4 us (5%)
  matrix products  1.32 us (2%)
  between operations  0.91 us (1%)
    all_gather x1, blocking collectives, body(): whole = lax.all_gather(replica, ('beam', 'pulse'), axis=1, tiled=True)  23.1 us
    gather x8, local copies, waits for them, and re-layouts, window(): return lax.dynamic_slice_in_dim(block, start, length, 1)  11.1 us
    ppermute x1, starting transfers between devices, padded_2(): lax.ppermute(tail, axis, [(i, (i + 1) % count) for i in range(ends)])  4.67 us
    gather x8, local copies, waits for them, and re-layouts  3.94 us
    another operation x4, other arithmetic  3.57 us
    ppermute x1, waiting for transfers between devices, padded_2(): lax.ppermute(head, axis, [((i + 1) % count, i) for i in range(ends)])  3.4 us
    unnamed x16, local copies, waits for them, and re-layouts  3.09 us
    another operation x4, local copies, waits for them, and re-layouts, skewed(): flat = jnp.tile(padded, TILE)[:TILE * width]  1.53 us
  transfers between devices with their start and end apart: 3, of which 1 were waited for; matrix products, arithmetic and copies ran while one was open for 6% of the time, Pallas kernels for 0%

commit v1 on v0

v1 whole, which is shorter than its diff:
```python
import functools

import jax
import jax.numpy as jnp
from jax import lax
from jax.experimental import pallas as pl
from jax.experimental.pallas import tpu as pltpu
from jax.sharding import PartitionSpec as P

TILE = 128
OFF_MAX = 128
EPSILON = 1e-06
MESH = pl.DeviceIdType.MESH


def plan(signal, replica, sizes):
    nb, npulse, nr = sizes
    pieces = nb * npulse
    piece = replica[1]
    gates = signal[3]
    total = gates * nr
    taps = min(piece * pieces, total)
    senders = -(-taps // piece)
    tiles = gates // TILE + 2
    panels = min(-(-piece * pieces // TILE) + 1, total // TILE)
    chunks = min(tiles + panels - 1, total // TILE + 1)
    beyond = (chunks - 1) * TILE - gates + OFF_MAX
    reach = min(-(-beyond // gates), nr - 1)
    keeps = [min(gates, beyond - s * gates) for s in range(reach)]
    return pieces, piece, gates, total, senders, tiles, panels, chunks, keeps


def kernel(
    sizes, dims, offsets, guards, trains, scales, sig, rep, comp, ratio, *scratch
):
    pieces, piece, gates, total, senders, tiles, panels, chunks, keeps = dims
    nb, npulse, nr = sizes
    beams, pulses = sig.shape[0], sig.shape[1]
    rows = beams * pulses
    hbuf, left, xf, xa, yf, hsend, hrecv, xsend, xrecv = scratch[:9]
    right = scratch[9:]
    bi, pi, ri = lax.axis_index("beam"), lax.axis_index("pulse"), lax.axis_index("range")
    me = bi * npulse + pi
    reach = len(keeps)

    def where_is(index):
        return {"beam": index // npulse, "pulse": index % npulse}

    barrier = pltpu.get_barrier_semaphore()
    for s in range(senders):

        @pl.when(me != s)
        def _():
            pl.semaphore_signal(
                barrier, inc=1, device_id=where_is(s), device_id_type=MESH
            )

    for s in range(1, reach + 1):

        @pl.when(ri + s < nr)
        def _():
            pl.semaphore_signal(
                barrier, inc=1, device_id={"range": ri + s}, device_id_type=MESH
            )

    @pl.when(ri >= 1)
    def _():
        pl.semaphore_signal(
            barrier, inc=1, device_id={"range": ri - 1}, device_id_type=MESH
        )

    def head_copy(s):
        return pltpu.make_async_remote_copy(
            src_ref=sig.at[:, :, :, pl.ds(0, keeps[s - 1])],
            dst_ref=right[s - 1],
            send_sem=xsend.at[s],
            recv_sem=xrecv.at[s],
            device_id={"range": ri - s},
            device_id_type=MESH,
        )

    def tail_copy():
        return pltpu.make_async_remote_copy(
            src_ref=sig.at[:, :, :, pl.ds(gates - TILE, TILE)],
            dst_ref=left,
            send_sem=xsend.at[0],
            recv_sem=xrecv.at[0],
            device_id={"range": ri + 1},
            device_id_type=MESH,
        )

    def tap_copy(slot, step, target):
        return pltpu.make_async_remote_copy(
            src_ref=rep,
            dst_ref=hbuf.at[slot],
            send_sem=hsend.at[step],
            recv_sem=hrecv.at[slot],
            device_id=where_is(target),
            device_id_type=MESH,
        )

    expect = jnp.minimum(ri, reach) + jnp.where(ri + 1 < nr, 1, 0)
    pl.semaphore_wait(barrier, expect + jnp.where(me < senders, pieces - 1, 0))

    @pl.when(me < senders)
    def _():
        for step in range(pieces - 1, 0, -1):
            tap_copy(me, step, lax.rem(me + step, pieces)).start()

    for s in range(1, reach + 1):

        @pl.when(ri - s >= 0)
        def _():
            head_copy(s).start()

    @pl.when(ri + 1 < nr)
    def _():
        tail_copy().start()

    @pl.when(me < senders)
    def _():
        hbuf[me] = rep[...]

    def place(source, start, width):
        for b in range(beams):
            for p in range(pulses):
                at = 2 * (b * pulses + p)
                pair = source[b, p].astype(jnp.float32)
                for c in range(width // TILE):
                    xf[start // TILE + c, at : at + 2, :] = pair[:, c * TILE : (c + 1) * TILE]

    def clear(start, stop):
        for c in range(start // TILE, stop // TILE):
            xf[c] = jnp.zeros((2 * rows, TILE), jnp.float32)

    place(sig, TILE, gates)
    tail = TILE + gates + sum(keeps)
    width = yf.shape[1]
    clear(tail, width)

    across = tiles - 2
    lane = lax.broadcasted_iota(jnp.int32, (TILE, 3 * TILE), 1)
    row = lax.broadcasted_iota(jnp.int32, (TILE, 3 * TILE), 0)
    apart = jnp.abs(lane - TILE - row)
    position = ri * gates + lax.broadcasted_iota(jnp.int32, (pulses, gates), 1)
    weights, counts, factors = [], [], []
    for b in range(beams):
        guard, train = guards[b], trains[b]
        inside = (apart > guard) & (apart <= guard + train)
        weights.append(jnp.where(inside, 1.0, 0.0).astype(jnp.bfloat16))
        count = jnp.clip(position - guard, 0, train) + jnp.clip(
            total - 1 - position - guard, 0, train
        )
        counts.append(count.astype(jnp.float32))
        level = jnp.full((pulses, TILE), scales[b], jnp.int32).astype(jnp.float32)
        factors.append(jnp.exp2(level / 8.0))

    @pl.when(ri >= 1)
    def _():
        tail_copy().wait_recv()
        place(left, 0, TILE)

    @pl.when(ri == 0)
    def _():
        clear(0, TILE)

    at = TILE + gates
    for s in range(1, reach + 1):
        start, keep = at, keeps[s - 1]

        @pl.when(ri + s < nr)
        def _():
            head_copy(s).wait_recv()
            place(right[s - 1], start, keep)

        @pl.when(ri + s >= nr)
        def _():
            clear(start, start + keep)

        at += keep

    for b in range(beams):
        low = 2 * b * pulses
        real, imag = [
            pltpu.roll(
                jnp.concatenate(
                    [
                        xf[c, pl.ds(low + part, pulses, stride=2), :]
                        for c in range(width // TILE)
                    ],
                    axis=1,
                ),
                width - offsets[b],
                1,
            )
            for part in range(2)
        ]
        yf[b * pulses : (b + 1) * pulses, :] = real
        yf[rows + b * pulses : rows + (b + 1) * pulses, :] = imag
    for c in range(chunks):
        real = yf[:rows, c * TILE : (c + 1) * TILE]
        imag = yf[rows:, c * TILE : (c + 1) * TILE]
        first = jnp.concatenate([real, imag], axis=1)
        second = jnp.concatenate([imag, -real], axis=1)
        xa[c] = jnp.concatenate([first, second], axis=0).astype(jnp.bfloat16)

    for s in range(senders):

        @pl.when(me != s)
        def _():
            tap_copy(s, 0, me).wait_recv()

    per = TILE // piece if piece < TILE else 1
    spread = max(piece // TILE, 1)

    def taps_of(c):
        if piece >= TILE:
            return hbuf[c // spread].astype(jnp.float32)[
                :, (c % spread) * TILE : (c % spread + 1) * TILE
            ]
        parts = [hbuf[c * per + i].astype(jnp.float32) for i in range(per)]
        return jnp.concatenate(parts, axis=1)

    held = min(panels, (senders * piece) // TILE)
    lane = lax.broadcasted_iota(jnp.int32, (TILE, TILE), 1)
    row = lax.broadcasted_iota(jnp.int32, (TILE, TILE), 0)
    ahead = lane >= row

    def skewed(values):
        flat = jnp.broadcast_to(values, (TILE, TILE))
        return pltpu.roll(flat, 0, 1, stride=1, stride_axis=0)

    zero = jnp.zeros((TILE, TILE), jnp.float32)
    before = (zero, zero)
    sums = [None] * tiles
    for c in range(panels):
        if c < held:
            taps = taps_of(c)
            now = (skewed(taps[0:1]), skewed(taps[1:2]))
        else:
            now = (zero, zero)
        panel = jnp.concatenate(
            [jnp.where(ahead, n, b) for n, b in zip(now, before)], axis=1
        ).astype(jnp.bfloat16)
        before = now
        n = min(tiles, chunks - c)
        left_side = xa[c : c + n].reshape(n * 2 * rows, 2 * TILE)
        product = lax.dot_general(
            left_side, panel, (((1,), (1,)), ((), ())), preferred_element_type=jnp.float32
        )
        for i in range(n):
            part = product[i * 2 * rows : (i + 1) * 2 * rows]
            sums[i] = part if sums[i] is None else sums[i] + part

    powers = []
    for i in range(tiles):
        rounded = sums[i].astype(jnp.bfloat16).astype(jnp.float32)
        real, imag = rounded[:rows], rounded[rows:]
        power = real * real + imag * imag
        if i == 0:
            power = jnp.where(ri >= 1, power, 0.0)
        powers.append(power)
        if 1 <= i <= across:
            xf[i - 1, pl.ds(0, rows, stride=2), :] = real
            xf[i - 1, pl.ds(1, rows, stride=2), :] = imag
    for b in range(beams):
        for p in range(pulses):
            at = 2 * (b * pulses + p)
            for i in range(across):
                comp[b, p, :, i * TILE : (i + 1) * TILE] = xf[i, at : at + 2, :].astype(
                    jnp.bfloat16
                )

    split = []
    for power in powers:
        high = power.astype(jnp.bfloat16)
        rest = power - high.astype(jnp.float32)
        middle = rest.astype(jnp.bfloat16)
        low = (rest - middle.astype(jnp.float32)).astype(jnp.bfloat16)
        split.append([v.astype(jnp.float32) for v in (high, middle, low)])
    for b in range(beams):
        mine = slice(b * pulses, (b + 1) * pulses)
        side = jnp.concatenate(
            [
                jnp.concatenate([split[i + d][k][mine] for d in range(3)], axis=1)
                for i in range(across)
                for k in range(3)
            ],
            axis=0,
        ).astype(jnp.bfloat16)
        window = lax.dot_general(
            side, weights[b], (((1,), (1,)), ((), ())), preferred_element_type=jnp.float32
        )
        for i in range(across):
            base = 3 * i * pulses
            noise = (
                window[base : base + pulses]
                + window[base + pulses : base + 2 * pulses]
                + window[base + 2 * pulses : base + 3 * pulses]
            ) / counts[b][:, i * TILE : (i + 1) * TILE]
            ratio[b, :, i * TILE : (i + 1) * TILE] = powers[i + 1][mine] / (
                factors[b] * (noise + EPSILON)
            )

    @pl.when(me < senders)
    def _():
        for step in range(1, pieces):
            tap_copy(me, step, me).wait_send()

    for s in range(1, reach + 1):

        @pl.when(ri - s >= 0)
        def _():
            head_copy(s).wait_send()

    @pl.when(ri + 1 < nr)
    def _():
        tail_copy().wait_send()


def body(sizes, signal, replica, guard_cells, train_cells, scale_index, offsets):
    dims = plan(signal.shape, replica.shape, sizes)
    pieces, piece, gates, total, senders, tiles, panels, chunks, keeps = dims
    beams, pulses = signal.shape[0], signal.shape[1]
    rows = beams * pulses
    width = max(chunks * TILE + OFF_MAX, TILE + gates + sum(keeps))
    smem = pl.BlockSpec(memory_space=pltpu.SMEM)
    vmem = pl.BlockSpec(memory_space=pltpu.VMEM)
    return pl.pallas_call(
        functools.partial(kernel, sizes, dims),
        out_shape=(
            jax.ShapeDtypeStruct(signal.shape, jnp.bfloat16),
            jax.ShapeDtypeStruct((beams, pulses, gates), jnp.float32),
        ),
        in_specs=[smem] * 4 + [vmem] * 2,
        out_specs=(vmem, vmem),
        scratch_shapes=[
            pltpu.VMEM((senders, 2, piece), jnp.bfloat16),
            pltpu.VMEM((beams, pulses, 2, TILE), jnp.bfloat16),
            pltpu.VMEM((width // TILE, 2 * rows, TILE), jnp.float32),
            pltpu.VMEM((chunks, 2 * rows, 2 * TILE), jnp.bfloat16),
            pltpu.VMEM((2 * rows, width), jnp.float32),
            pltpu.SemaphoreType.DMA((pieces,)),
            pltpu.SemaphoreType.DMA((senders,)),
            pltpu.SemaphoreType.DMA((len(keeps) + 1,)),
            pltpu.SemaphoreType.DMA((len(keeps) + 1,)),
        ]
        + [pltpu.VMEM((beams, pulses, 2, keep), jnp.bfloat16) for keep in keeps],
        compiler_params=pltpu.CompilerParams(collective_id=0, has_side_effects=True),
    )(offsets, guard_cells, train_cells, scale_index, signal, replica)


def solution(mesh):
    placed = (
        P("beam", "pulse", None, "range"),
        P(None, ("beam", "pulse")),
        P("beam"),
        P("beam"),
        P("beam"),
        P("beam"),
    )
    sizes = (mesh.shape["beam"], mesh.shape["pulse"], mesh.shape["range"])
    return jax.shard_map(
        functools.partial(body, sizes),
        mesh=mesh,
        in_specs=placed,
        out_specs=(P("beam", "pulse", None, "range"), P("beam", "pulse", "range")),
        check_vma=False,
    )
```

time: 62.8 us -> 14.9 us (0.24)
  blocking collectives: 23.1 us -> 0 us
  local copies, waits for them, and re-layouts: 21.7 us -> 2.02 us
  Pallas kernels: 0 us -> 12 us
  starting transfers between devices: 7.43 us -> 0 us
  other arithmetic: 4.6 us -> 0 us
  waiting for transfers between devices: 3.4 us -> 0 us
  matrix products: 1.32 us -> 0 us
    all_gather x1 -> x0, blocking collectives: 23.1 us -> none  [body(): whole = lax.all_gather(replica, ('beam', 'pulse'), axis=1, tiled=True)]
    gather x16 -> x0, local copies, waits for them, and re-layouts: 15.1 us -> none  [the longest x8 11.1 us: window(): return lax.dynamic_slice_in_dim(block, start, length, 1)]
    pallas_call x0 -> x1, Pallas kernels: none -> 12 us  [body(): pl.pallas_call(functools.partial(kernel, sizes, dims), out_shape=(jax.Sha...]
    ppermute x3 -> x0, starting transfers between devices: 7.43 us -> none  [the longest x1 4.67 us: padded_2(): lax.ppermute(tail, axis, [(i, (i + 1) % count) for i in range(ends)])]
    another operation x5 -> x0, other arithmetic: 3.65 us -> none
    ppermute x3 -> x0, waiting for transfers between devices: 3.4 us -> none  [the longest x1 3.4 us: padded_2(): lax.ppermute(head, axis, [((i + 1) % count, i) for i in range(ends)])]
    another operation x9 -> x0, local copies, waits for them, and re-layouts: 1.79 us -> none  [the longest x4 1.53 us: skewed(): flat = jnp.tile(padded, TILE)[:TILE * width]]
    dot_general x4 -> x0, matrix products: 1.32 us -> none  [the longest x1 0.33 us: block_fn(): lax.dot_general(real_part, panel_imag, dims, preferred_element_type=jnp.f...]
  transfers between devices with their start and end apart: 3 -> 0, of which waited for: 1 -> 0; matrix products, arithmetic and copies ran while one was open for 6% -> 0% of each run, Pallas kernels for 0% -> 0%
where the time goes in v1:
time: 14.9 us; the launch traced here: 14.7 us
  Pallas kernels  12 us (81%)
  local copies, waits for them, and re-layouts  2.02 us (14%)
  between operations  0.65 us (4%)
    pallas_call x1, Pallas kernels, body(): pl.pallas_call(functools.partial(kernel, sizes, dims), out_shape=(jax.Sha...  12 us
    unnamed x4, local copies, waits for them, and re-layouts  2.02 us

profile of v1, /device:TPU:0, one launch (start us, length us, event | category | flops | bytes accessed | tf_op | source)
XLA Modules:
  0.0 14.7 jit_solution(2518699682888872360)
XLA Ops:
  0.6 12.0 %shard_map.77 = (bf16[2,8,2,512]{3,2,1,0:T(2,128)(2,1)}, f32[2,8,512]{2,1,0:T(8,128)}) custom-call(s32[2]{0:T(128)} %offsets.1, s32[2]{0:T(128)} %guards.1, s32[2]{0:T(128)} %trains.1, s32[2]{0:T(128)} %scales.1, bf16[2,8,2,512]{3,2,1,0:T(2,128)(2,1)} %sig.1, bf16[2,128]{1,0:T(2,128)(2,1)} %rep.1), custom_call_target="tpu_custom_call" | custom-call | tf_op jit(solution)/shard_map/pallas_call | solution.py:329
  12.6 0.0 copy-start
  12.6 1.4 %copy.10 = bf16[2,8,2,512]{3,2,1,0:T(2,128)(2,1)} copy(bf16[2,8,2,512]{3,2,1,0:T(2,128)(2,1)} %get-tuple-element.4) | data formatting | bytes 65536
  14.0 0.0 copy-done
  14.0 0.6 %copy.11 = f32[2,8,512]{2,1,0:T(8,128)} copy(f32[2,8,512]{2,1,0:T(8,128)S(1)} %copy-done) | data formatting | bytes 65536
Async XLA Ops:
  12.6 1.4 %copy-start = (f32[2,8,512]{2,1,0:T(8,128)S(1)}, f32[2,8,512]{2,1,0:T(8,128)}, u32[]{:S(2)}) copy-start(f32[2,8,512]{2,1,0:T(8,128)} %get-tuple-element.5) | copy-start | bytes 98308

commit v2 on v1

--- a/solution.py
+++ b/solution.py
@@ -10,6 +10,7 @@
 TILE = 128
 OFF_MAX = 128
 EPSILON = 1e-06
+GRANT = 24 << 20
 MESH = pl.DeviceIdType.MESH
 
 
@@ -30,15 +31,17 @@
     return pieces, piece, gates, total, senders, tiles, panels, chunks, keeps
 
 
-def kernel(
-    sizes, dims, offsets, guards, trains, scales, sig, rep, comp, ratio, *scratch
-):
+def gather(sizes, dims, *refs):
     pieces, piece, gates, total, senders, tiles, panels, chunks, keeps = dims
     nb, npulse, nr = sizes
+    numbers, (sig, rep) = refs[:4], refs[4:6]
+    hout, xa, weights, counts, factors = refs[6:11]
+    hbuf, own, left, xf, yf = refs[11:16]
+    offsets, guards, trains, scales = refs[16:20]
+    here, hsend, hrecv, xsend, xrecv = refs[20:25]
+    right = refs[25:]
     beams, pulses = sig.shape[0], sig.shape[1]
     rows = beams * pulses
-    hbuf, left, xf, xa, yf, hsend, hrecv, xsend, xrecv = scratch[:9]
-    right = scratch[9:]
     bi, pi, ri = lax.axis_index("beam"), lax.axis_index("pulse"), lax.axis_index("range")
     me = bi * npulse + pi
     reach = len(keeps)
@@ -68,6 +71,12 @@
         pl.semaphore_signal(
             barrier, inc=1, device_id={"range": ri - 1}, device_id_type=MESH
         )
+
+    local = [pltpu.make_async_copy(sig, own, here.at[0])]
+    for n, (number, kept) in enumerate(zip(numbers, (offsets, guards, trains, scales))):
+        local.append(pltpu.make_async_copy(number, kept, here.at[n + 1]))
+    for copy in local:
+        copy.start()
 
     def head_copy(s):
         return pltpu.make_async_remote_copy(
@@ -117,9 +126,12 @@
     def _():
         tail_copy().start()
 
+    def own_taps():
+        return pltpu.make_async_copy(rep, hbuf.at[me], here.at[5])
+
     @pl.when(me < senders)
     def _():
-        hbuf[me] = rep[...]
+        own_taps().start()
 
     def place(source, start, width):
         for b in range(beams):
@@ -133,27 +145,27 @@
         for c in range(start // TILE, stop // TILE):
             xf[c] = jnp.zeros((2 * rows, TILE), jnp.float32)
 
-    place(sig, TILE, gates)
+    for copy in local:
+        copy.wait()
+    place(own, TILE, gates)
     tail = TILE + gates + sum(keeps)
     width = yf.shape[1]
     clear(tail, width)
 
-    across = tiles - 2
     lane = lax.broadcasted_iota(jnp.int32, (TILE, 3 * TILE), 1)
     row = lax.broadcasted_iota(jnp.int32, (TILE, 3 * TILE), 0)
     apart = jnp.abs(lane - TILE - row)
     position = ri * gates + lax.broadcasted_iota(jnp.int32, (pulses, gates), 1)
-    weights, counts, factors = [], [], []
     for b in range(beams):
         guard, train = guards[b], trains[b]
         inside = (apart > guard) & (apart <= guard + train)
-        weights.append(jnp.where(inside, 1.0, 0.0).astype(jnp.bfloat16))
+        weights[b] = jnp.where(inside, 1.0, 0.0).astype(jnp.bfloat16)
         count = jnp.clip(position - guard, 0, train) + jnp.clip(
             total - 1 - position - guard, 0, train
         )
-        counts.append(count.astype(jnp.float32))
+        counts[b] = count.astype(jnp.float32)
         level = jnp.full((pulses, TILE), scales[b], jnp.int32).astype(jnp.float32)
-        factors.append(jnp.exp2(level / 8.0))
+        factors[b] = jnp.exp2(level / 8.0)
 
     @pl.when(ri >= 1)
     def _():
@@ -204,21 +216,51 @@
         second = jnp.concatenate([imag, -real], axis=1)
         xa[c] = jnp.concatenate([first, second], axis=0).astype(jnp.bfloat16)
 
+    @pl.when(me < senders)
+    def _():
+        own_taps().wait()
+
     for s in range(senders):
 
         @pl.when(me != s)
         def _():
             tap_copy(s, 0, me).wait_recv()
+
+    hout[...] = hbuf[...]
+
+    @pl.when(me < senders)
+    def _():
+        for step in range(1, pieces):
+            tap_copy(me, step, me).wait_send()
+
+    for s in range(1, reach + 1):
+
+        @pl.when(ri - s >= 0)
+        def _():
+            head_copy(s).wait_send()
+
+    @pl.when(ri + 1 < nr)
+    def _():
+        tail_copy().wait_send()
+
+
+def compute(sizes, dims, taps_ref, xa, weights, counts, factors, comp, ratio, xf):
+    pieces, piece, gates, total, senders, tiles, panels, chunks, keeps = dims
+    beams, pulses = comp.shape[0], comp.shape[1]
+    rows = beams * pulses
+    ri = lax.axis_index("range")
+
+    across = tiles - 2
 
     per = TILE // piece if piece < TILE else 1
     spread = max(piece // TILE, 1)
 
     def taps_of(c):
         if piece >= TILE:
-            return hbuf[c // spread].astype(jnp.float32)[
+            return taps_ref[c // spread].astype(jnp.float32)[
                 :, (c % spread) * TILE : (c % spread + 1) * TILE
             ]
-        parts = [hbuf[c * per + i].astype(jnp.float32) for i in range(per)]
+        parts = [taps_ref[c * per + i].astype(jnp.float32) for i in range(per)]
         return jnp.concatenate(parts, axis=1)
 
     held = min(panels, (senders * piece) // TILE)
@@ -297,25 +339,10 @@
                 window[base : base + pulses]
                 + window[base + pulses : base + 2 * pulses]
                 + window[base + 2 * pulses : base + 3 * pulses]
-            ) / counts[b][:, i * TILE : (i + 1) * TILE]
+            ) / counts[b, :, i * TILE : (i + 1) * TILE]
             ratio[b, :, i * TILE : (i + 1) * TILE] = powers[i + 1][mine] / (
                 factors[b] * (noise + EPSILON)
             )
-
-    @pl.when(me < senders)
-    def _():
-        for step in range(1, pieces):
-            tap_copy(me, step, me).wait_send()
-
-    for s in range(1, reach + 1):
-
-        @pl.when(ri - s >= 0)
-        def _():
-            head_copy(s).wait_send()
-
-    @pl.when(ri + 1 < nr)
-    def _():
-        tail_copy().wait_send()
 
 
 def body(sizes, signal, replica, guard_cells, train_cells, scale_index, offsets):
@@ -324,30 +351,54 @@
     beams, pulses = signal.shape[0], signal.shape[1]
     rows = beams * pulses
     width = max(chunks * TILE + OFF_MAX, TILE + gates + sum(keeps))
-    smem = pl.BlockSpec(memory_space=pltpu.SMEM)
     vmem = pl.BlockSpec(memory_space=pltpu.VMEM)
+    placed = pl.BlockSpec(memory_space=pltpu.HBM)
+    reach = len(keeps)
+    operands = (offsets, guard_cells, train_cells, scale_index, signal, replica)
+    gathered = pl.pallas_call(
+        functools.partial(gather, sizes, dims),
+        out_shape=(
+            jax.ShapeDtypeStruct((senders, 2, piece), jnp.bfloat16),
+            jax.ShapeDtypeStruct((chunks, 2 * rows, 2 * TILE), jnp.bfloat16),
+            jax.ShapeDtypeStruct((beams, TILE, 3 * TILE), jnp.bfloat16),
+            jax.ShapeDtypeStruct((beams, pulses, gates), jnp.float32),
+            jax.ShapeDtypeStruct((beams, pulses, TILE), jnp.float32),
+        ),
+        in_specs=[placed] * 6,
+        out_specs=(vmem,) * 5,
+        scratch_shapes=[
+            pltpu.VMEM((senders, 2, piece), jnp.bfloat16),
+            pltpu.VMEM(signal.shape, jnp.bfloat16),
+            pltpu.VMEM((beams, pulses, 2, TILE), jnp.bfloat16),
+            pltpu.VMEM((width // TILE, 2 * rows, TILE), jnp.float32),
+            pltpu.VMEM((2 * rows, width), jnp.float32),
+        ]
+        + [pltpu.SMEM((beams,), jnp.int32)] * 4
+        + [
+            pltpu.SemaphoreType.DMA((6,)),
+            pltpu.SemaphoreType.DMA((pieces,)),
+            pltpu.SemaphoreType.DMA((senders,)),
+            pltpu.SemaphoreType.DMA((reach + 1,)),
+            pltpu.SemaphoreType.DMA((reach + 1,)),
+        ]
+        + [pltpu.VMEM((beams, pulses, 2, keep), jnp.bfloat16) for keep in keeps],
+        compiler_params=pltpu.CompilerParams(
+            collective_id=0, has_side_effects=True, vmem_limit_bytes=GRANT
+        ),
+        name="gather",
+    )(*[pltpu.with_memory_space_constraint(v, pltpu.HBM) for v in operands])
     return pl.pallas_call(
-        functools.partial(kernel, sizes, dims),
+        functools.partial(compute, sizes, dims),
         out_shape=(
             jax.ShapeDtypeStruct(signal.shape, jnp.bfloat16),
             jax.ShapeDtypeStruct((beams, pulses, gates), jnp.float32),
         ),
-        in_specs=[smem] * 4 + [vmem] * 2,
+        in_specs=[vmem] * 5,
         out_specs=(vmem, vmem),
-        scratch_shapes=[
-            pltpu.VMEM((senders, 2, piece), jnp.bfloat16),
-            pltpu.VMEM((beams, pulses, 2, TILE), jnp.bfloat16),
-            pltpu.VMEM((width // TILE, 2 * rows, TILE), jnp.float32),
-            pltpu.VMEM((chunks, 2 * rows, 2 * TILE), jnp.bfloat16),
-            pltpu.VMEM((2 * rows, width), jnp.float32),
-            pltpu.SemaphoreType.DMA((pieces,)),
-            pltpu.SemaphoreType.DMA((senders,)),
-            pltpu.SemaphoreType.DMA((len(keeps) + 1,)),
-            pltpu.SemaphoreType.DMA((len(keeps) + 1,)),
-        ]
-        + [pltpu.VMEM((beams, pulses, 2, keep), jnp.bfloat16) for keep in keeps],
-        compiler_params=pltpu.CompilerParams(collective_id=0, has_side_effects=True),
-    )(offsets, guard_cells, train_cells, scale_index, signal, replica)
+        scratch_shapes=[pltpu.VMEM((gates // TILE, 2 * rows, TILE), jnp.float32)],
+        compiler_params=pltpu.CompilerParams(vmem_limit_bytes=GRANT),
+        name="compute",
+    )(*gathered)
 
 
 def solution(mesh):

time: 14.9 us -> 12.3 us (0.83)
  local copies, waits for them, and re-layouts: 2.02 us -> 0 us
  Pallas kernels: 12 us -> 11.5 us
    unnamed x4 -> x0, local copies, waits for them, and re-layouts: 2.02 us -> none
    pallas_call x1 -> x2, Pallas kernels: 12 us -> 11.5 us  [the longest x1 10.2 us: body(): pl.pallas_call(functools.partial(gather, sizes, dims), out_shape=(jax.Sha...]
where the time goes in v2:
time: 12.3 us; the launch traced here: 12.1 us
  Pallas kernels  11.5 us (93%)
  between operations  0.64 us (5%)
    pallas_call x1, Pallas kernels, body(): pl.pallas_call(functools.partial(gather, sizes, dims), out_shape=(jax.Sha...  10.2 us
    pallas_call x1, Pallas kernels, body(): pl.pallas_call(functools.partial(compute, sizes, dims), out_shape=(jax.Sh...  1.34 us

profile of v2, /device:TPU:0, one launch (start us, length us, event | category | flops | bytes accessed | tf_op | source)
XLA Modules:
  0.0 12.1 jit_solution(12303691368167228850)
XLA Ops:
  0.6 10.2 %gather.1 = (bf16[8,2,128]{2,1,0:T(2,128)(2,1)S(1)}, bf16[9,32,256]{2,1,0:T(8,128)(2,1)S(1)}, bf16[2,128,384]{2,1,0:T(8,128)(2,1)S(1)}, f32[2,8,512]{2,1,0:T(8,128)S(1)}, f32[2,8,128]{2,1,0:T(8,128)S(1)}) custom-call(s32[2]{0:T(128)} %refs_0_.1, s32[2]{0:T(128)} %refs_1_.1, s32[2]{0:T(128)} %refs_2_.1, s32[2]{0:T(128)} %refs_3_.1, ...), custom_call_target="tpu_custom_call" | custom-call | tf_op jit(solution)/shard_map/gather/pallas_call | solution.py:358
  10.8 1.3 %compute.1 = (bf16[2,8,2,512]{3,2,1,0:T(2,128)(2,1)}, f32[2,8,512]{2,1,0:T(8,128)}) custom-call(bf16[8,2,128]{2,1,0:T(2,128)(2,1)S(1)} %get-tuple-element.7.taps_ref, bf16[9,32,256]{2,1,0:T(8,128)(2,1)S(1)} %get-tuple-element.8.xa, bf16[2,128,384]{2,1,0:T(8,128)(2,1)S(1)} %get-tuple-element.9.weights, f32[2,8,512]{2,1,0:T(8,128)S(1)} %get-tuple-element.10.counts, ...), custom_call_target="tpu_custom_call" | custom-call | tf_op jit(solution)/shard_map/compute/pallas_call | solution.py:390

commit v3 on v2

--- a/solution.py
+++ b/solution.py
@@ -21,7 +21,7 @@
     gates = signal[3]
     total = gates * nr
     taps = min(piece * pieces, total)
-    senders = -(-taps // piece)
+    senders = -(-taps // (piece * npulse)) * npulse
     tiles = gates // TILE + 2
     panels = min(-(-piece * pieces // TILE) + 1, total // TILE)
     chunks = min(tiles + panels - 1, total // TILE + 1)
@@ -38,25 +38,34 @@
     hout, xa, weights, counts, factors = refs[6:11]
     hbuf, own, left, xf, yf = refs[11:16]
     offsets, guards, trains, scales = refs[16:20]
-    here, hsend, hrecv, xsend, xrecv = refs[20:25]
-    right = refs[25:]
+    here, hsend, hrecv, xsend, xrecv, ready = refs[20:26]
+    right = refs[26:]
     beams, pulses = sig.shape[0], sig.shape[1]
     rows = beams * pulses
     bi, pi, ri = lax.axis_index("beam"), lax.axis_index("pulse"), lax.axis_index("range")
     me = bi * npulse + pi
+    planes = senders // npulse
     reach = len(keeps)
 
-    def where_is(index):
-        return {"beam": index // npulse, "pulse": index % npulse}
+    def say(semaphore, plane, pulse):
+        pl.semaphore_signal(
+            semaphore,
+            inc=1,
+            device_id={"beam": plane, "pulse": pulse},
+            device_id_type=MESH,
+        )
 
     barrier = pltpu.get_barrier_semaphore()
-    for s in range(senders):
-
-        @pl.when(me != s)
-        def _():
-            pl.semaphore_signal(
-                barrier, inc=1, device_id=where_is(s), device_id_type=MESH
-            )
+
+    @pl.when(bi + 1 < nb)
+    def _():
+        for j in range(npulse):
+            say(barrier, bi + 1, j)
+
+    @pl.when(bi < planes)
+    def _():
+        for j in range(1, npulse):
+            say(barrier, bi, lax.rem(pi + j, npulse))
 
     for s in range(1, reach + 1):
 
@@ -98,23 +107,48 @@
             device_id_type=MESH,
         )
 
-    def tap_copy(slot, step, target):
-        return pltpu.make_async_remote_copy(
-            src_ref=rep,
-            dst_ref=hbuf.at[slot],
-            send_sem=hsend.at[step],
-            recv_sem=hrecv.at[slot],
-            device_id=where_is(target),
-            device_id_type=MESH,
-        )
+    def tap_copies(source, slot, way, plane):
+        return [
+            pltpu.make_async_remote_copy(
+                src_ref=source,
+                dst_ref=hbuf.at[slot],
+                send_sem=hsend.at[way, j],
+                recv_sem=hrecv.at[slot],
+                device_id={"beam": plane, "pulse": lax.rem(pi + j, npulse)},
+                device_id_type=MESH,
+            )
+            for j in range(1 if way == 0 else 0, npulse)
+        ]
+
+    def same_plane():
+        return tap_copies(rep, me, 0, bi)
+
+    def down(b, source):
+        return tap_copies(source, b * npulse + pi, 1 + b, bi - 1)
+
+    def up(b, source):
+        return tap_copies(source, b * npulse + pi, 1 + planes + b, bi + 1)
 
     expect = jnp.minimum(ri, reach) + jnp.where(ri + 1 < nr, 1, 0)
-    pl.semaphore_wait(barrier, expect + jnp.where(me < senders, pieces - 1, 0))
-
-    @pl.when(me < senders)
-    def _():
-        for step in range(pieces - 1, 0, -1):
-            tap_copy(me, step, lax.rem(me + step, pieces)).start()
+    expect += jnp.where(bi < planes, npulse - 1, 0) + jnp.where(bi >= 1, npulse, 0)
+    pl.semaphore_wait(barrier, expect)
+
+    @pl.when(bi >= 1)
+    def _():
+        for j in range(npulse):
+            say(ready, bi - 1, lax.rem(pi + j, npulse))
+
+    for b in range(planes):
+
+        @pl.when((bi == b) & (bi >= 1))
+        def _():
+            for copy in down(b, rep):
+                copy.start()
+
+    @pl.when(bi < planes)
+    def _():
+        for copy in same_plane():
+            copy.start()
 
     for s in range(1, reach + 1):
 
@@ -166,6 +200,16 @@
         counts[b] = count.astype(jnp.float32)
         level = jnp.full((pulses, TILE), scales[b], jnp.int32).astype(jnp.float32)
         factors[b] = jnp.exp2(level / 8.0)
+
+    @pl.when(bi + 1 < nb)
+    def _():
+        pl.semaphore_wait(ready, npulse)
+        for b in range(planes):
+
+            @pl.when(bi == b)
+            def _():
+                for copy in up(b, rep):
+                    copy.start()
 
     @pl.when(ri >= 1)
     def _():
@@ -220,18 +264,47 @@
     def _():
         own_taps().wait()
 
-    for s in range(senders):
-
-        @pl.when(me != s)
-        def _():
-            tap_copy(s, 0, me).wait_recv()
+    for b in reversed(range(planes)):
+
+        @pl.when(bi != b)
+        def _():
+            slot = b * npulse + pi
+            up(b, hbuf.at[slot])[0].wait_recv()
+
+            @pl.when((bi < b) & (bi >= 1))
+            def _():
+                for copy in down(b, hbuf.at[slot]):
+                    copy.start()
+
+            @pl.when((bi > b) & (bi + 1 < nb))
+            def _():
+                for copy in up(b, hbuf.at[slot]):
+                    copy.start()
+
+    for slot in range(senders):
+
+        @pl.when(pi != slot % npulse)
+        def _():
+            tap_copies(rep, slot, 1, 0)[0].wait_recv()
 
     hout[...] = hbuf[...]
 
     @pl.when(me < senders)
     def _():
-        for step in range(1, pieces):
-            tap_copy(me, step, me).wait_send()
+        for copy in same_plane():
+            copy.wait_send()
+
+    for b in range(planes):
+
+        @pl.when((bi <= b) & (bi >= 1))
+        def _():
+            for copy in down(b, rep):
+                copy.wait_send()
+
+        @pl.when((bi >= b) & (bi + 1 < nb))
+        def _():
+            for copy in up(b, rep):
+                copy.wait_send()
 
     for s in range(1, reach + 1):
 
@@ -376,10 +449,11 @@
         + [pltpu.SMEM((beams,), jnp.int32)] * 4
         + [
             pltpu.SemaphoreType.DMA((6,)),
-            pltpu.SemaphoreType.DMA((pieces,)),
+            pltpu.SemaphoreType.DMA((2 * (senders // sizes[1]) + 1, sizes[1])),
             pltpu.SemaphoreType.DMA((senders,)),
             pltpu.SemaphoreType.DMA((reach + 1,)),
             pltpu.SemaphoreType.DMA((reach + 1,)),
+            pltpu.SemaphoreType.REGULAR,
         ]
         + [pltpu.VMEM((beams, pulses, 2, keep), jnp.bfloat16) for keep in keeps],
         compiler_params=pltpu.CompilerParams(

time: 12.3 us -> 12.7 us (1.033)
  the two profiles are of different devices: /device:TPU:0 before, /device:TPU:24 now
where the time goes in v3:
time: 12.7 us; the launch traced here: 12.6 us
  Pallas kernels  11.9 us (94%)
  between operations  0.64 us (5%)
    pallas_call x1, Pallas kernels, body(): pl.pallas_call(functools.partial(gather, sizes, dims), out_shape=(jax.Sha...  10.6 us
    pallas_call x1, Pallas kernels, body(): pl.pallas_call(functools.partial(compute, sizes, dims), out_shape=(jax.Sh...  1.34 us

profile of v3, /device:TPU:24, one launch (start us, length us, event | category | flops | bytes accessed | tf_op | source)
XLA Modules:
  0.0 12.6 jit_solution(3529777544411744895)
XLA Ops:
  0.6 10.6 %gather.1 = (bf16[8,2,128]{2,1,0:T(2,128)(2,1)S(1)}, bf16[9,32,256]{2,1,0:T(8,128)(2,1)S(1)}, bf16[2,128,384]{2,1,0:T(8,128)(2,1)S(1)}, f32[2,8,512]{2,1,0:T(8,128)S(1)}, f32[2,8,128]{2,1,0:T(8,128)S(1)}) custom-call(s32[2]{0:T(128)} %refs_0_.1, s32[2]{0:T(128)} %refs_1_.1, s32[2]{0:T(128)} %refs_2_.1, s32[2]{0:T(128)} %refs_3_.1, ...), custom_call_target="tpu_custom_call" | custom-call | tf_op jit(solution)/shard_map/gather/pallas_call | solution.py:431
  11.3 1.3 %compute.1 = (bf16[2,8,2,512]{3,2,1,0:T(2,128)(2,1)}, f32[2,8,512]{2,1,0:T(8,128)}) custom-call(bf16[8,2,128]{2,1,0:T(2,128)(2,1)S(1)} %get-tuple-element.7.taps_ref, bf16[9,32,256]{2,1,0:T(8,128)(2,1)S(1)} %get-tuple-element.8.xa, bf16[2,128,384]{2,1,0:T(8,128)(2,1)S(1)} %get-tuple-element.9.weights, f32[2,8,512]{2,1,0:T(8,128)S(1)} %get-tuple-element.10.counts, ...), custom_call_target="tpu_custom_call" | custom-call | tf_op jit(solution)/shard_map/compute/pallas_call | solution.py:464

commit v4 on v3

--- a/solution.py
+++ b/solution.py
@@ -57,15 +57,23 @@
 
     barrier = pltpu.get_barrier_semaphore()
 
-    @pl.when(bi + 1 < nb)
-    def _():
-        for j in range(npulse):
-            say(barrier, bi + 1, j)
-
     @pl.when(bi < planes)
     def _():
         for j in range(1, npulse):
             say(barrier, bi, lax.rem(pi + j, npulse))
+
+    for side in (-1, 1):
+
+        @pl.when((bi < planes) & (bi + side >= 0) & (bi + side < planes))
+        def _():
+            for j in range(npulse):
+                say(barrier, bi + side, lax.rem(pi + j, npulse))
+
+    @pl.when(bi == planes - 1)
+    def _():
+        for q in range(planes, nb):
+            for j in range(npulse):
+                say(barrier, q, lax.rem(pi + j, npulse))
 
     for s in range(1, reach + 1):
 
@@ -129,26 +137,45 @@
     def up(b, source):
         return tap_copies(source, b * npulse + pi, 1 + planes + b, bi + 1)
 
+    def beyond(b, source, q):
+        way = 1 + (2 + q - planes) * planes + b
+        return tap_copies(source, b * npulse + pi, way, q)
+
+    def arrived(slot):
+        copy = pltpu.make_async_remote_copy(
+            src_ref=rep,
+            dst_ref=hbuf.at[slot],
+            send_sem=hsend.at[0, 0],
+            recv_sem=hrecv.at[slot],
+            device_id={"beam": bi},
+            device_id_type=MESH,
+        )
+        copy.wait_recv()
+
     expect = jnp.minimum(ri, reach) + jnp.where(ri + 1 < nr, 1, 0)
-    expect += jnp.where(bi < planes, npulse - 1, 0) + jnp.where(bi >= 1, npulse, 0)
+    beside = jnp.where(bi >= 1, npulse, 0) + jnp.where(bi + 1 < planes, npulse, 0)
+    expect += jnp.where(bi < planes, npulse - 1 + beside, npulse)
     pl.semaphore_wait(barrier, expect)
 
-    @pl.when(bi >= 1)
-    def _():
-        for j in range(npulse):
-            say(ready, bi - 1, lax.rem(pi + j, npulse))
+    for q in range(planes, nb):
+
+        @pl.when(bi == q)
+        def _():
+            for j in range(npulse):
+                say(ready.at[q - planes], planes - 1, lax.rem(pi + j, npulse))
 
     for b in range(planes):
 
-        @pl.when((bi == b) & (bi >= 1))
-        def _():
-            for copy in down(b, rep):
+        @pl.when(bi == b)
+        def _():
+            if b >= 1:
+                for copy in down(b, rep):
+                    copy.start()
+            if b + 1 < planes:
+                for copy in up(b, rep):
+                    copy.start()
+            for copy in same_plane():
                 copy.start()
-
-    @pl.when(bi < planes)
-    def _():
-        for copy in same_plane():
-            copy.start()
 
     for s in range(1, reach + 1):
 
@@ -201,14 +228,30 @@
         level = jnp.full((pulses, TILE), scales[b], jnp.int32).astype(jnp.float32)
         factors[b] = jnp.exp2(level / 8.0)
 
-    @pl.when(bi + 1 < nb)
-    def _():
-        pl.semaphore_wait(ready, npulse)
-        for b in range(planes):
-
-            @pl.when(bi == b)
+    for b in reversed(range(planes)):
+
+        @pl.when((bi < planes) & (bi != b) & (bi >= 1))
+        def _():
+            slot = b * npulse + pi
+            arrived(slot)
+
+            @pl.when(bi < b)
             def _():
-                for copy in up(b, rep):
+                for copy in down(b, hbuf.at[slot]):
+                    copy.start()
+
+            @pl.when((bi > b) & (bi + 1 < planes))
+            def _():
+                for copy in up(b, hbuf.at[slot]):
+                    copy.start()
+
+    @pl.when(bi == planes - 1)
+    def _():
+        for q in range(planes, nb):
+            pl.semaphore_wait(ready.at[q - planes], npulse)
+            for b in range(planes):
+                source = rep if b == planes - 1 else hbuf.at[b * npulse + pi]
+                for copy in beyond(b, source, q):
                     copy.start()
 
     @pl.when(ri >= 1)
@@ -264,47 +307,39 @@
     def _():
         own_taps().wait()
 
-    for b in reversed(range(planes)):
-
-        @pl.when(bi != b)
-        def _():
-            slot = b * npulse + pi
-            up(b, hbuf.at[slot])[0].wait_recv()
-
-            @pl.when((bi < b) & (bi >= 1))
-            def _():
-                for copy in down(b, hbuf.at[slot]):
-                    copy.start()
-
-            @pl.when((bi > b) & (bi + 1 < nb))
-            def _():
-                for copy in up(b, hbuf.at[slot]):
-                    copy.start()
-
     for slot in range(senders):
 
-        @pl.when(pi != slot % npulse)
-        def _():
-            tap_copies(rep, slot, 1, 0)[0].wait_recv()
+        first = (bi == 0) & (slot >= npulse)
+
+        @pl.when((pi != slot % npulse) | (bi >= planes) | first)
+        def _():
+            arrived(slot)
 
     hout[...] = hbuf[...]
 
-    @pl.when(me < senders)
+    @pl.when(bi < planes)
     def _():
         for copy in same_plane():
             copy.wait_send()
 
     for b in range(planes):
 
-        @pl.when((bi <= b) & (bi >= 1))
+        @pl.when((bi < planes) & (bi <= b) & (bi >= 1))
         def _():
             for copy in down(b, rep):
                 copy.wait_send()
 
-        @pl.when((bi >= b) & (bi + 1 < nb))
+        @pl.when((bi >= b) & (bi + 1 < planes))
         def _():
             for copy in up(b, rep):
                 copy.wait_send()
+
+    @pl.when(bi == planes - 1)
+    def _():
+        for q in range(planes, nb):
+            for b in range(planes):
+                for copy in beyond(b, rep, q):
+                    copy.wait_send()
 
     for s in range(1, reach + 1):
 
@@ -427,6 +462,7 @@
     vmem = pl.BlockSpec(memory_space=pltpu.VMEM)
     placed = pl.BlockSpec(memory_space=pltpu.HBM)
     reach = len(keeps)
+    planes = senders // sizes[1]
     operands = (offsets, guard_cells, train_cells, scale_index, signal, replica)
     gathered = pl.pallas_call(
         functools.partial(gather, sizes, dims),
@@ -449,11 +485,11 @@
         + [pltpu.SMEM((beams,), jnp.int32)] * 4
         + [
             pltpu.SemaphoreType.DMA((6,)),
-            pltpu.SemaphoreType.DMA((2 * (senders // sizes[1]) + 1, sizes[1])),
+            pltpu.SemaphoreType.DMA((1 + planes * (2 + sizes[0] - planes), sizes[1])),
             pltpu.SemaphoreType.DMA((senders,)),
             pltpu.SemaphoreType.DMA((reach + 1,)),
             pltpu.SemaphoreType.DMA((reach + 1,)),
-            pltpu.SemaphoreType.REGULAR,
+            pltpu.SemaphoreType.REGULAR((max(sizes[0] - planes, 1),)),
         ]
         + [pltpu.VMEM((beams, pulses, 2, keep), jnp.bfloat16) for keep in keeps],
         compiler_params=pltpu.CompilerParams(

time: 12.7 us -> 10.5 us (0.83)
  the two profiles are of different devices: /device:TPU:24 before, /device:TPU:0 now
where the time goes in v4:
time: 10.5 us; the launch traced here: 10.4 us
  Pallas kernels  9.75 us (93%)
  between operations  0.64 us (6%)
    pallas_call x1, Pallas kernels, body(): pl.pallas_call(functools.partial(gather, sizes, dims), out_shape=(jax.Sha...  8.41 us
    pallas_call x1, Pallas kernels, body(): pl.pallas_call(functools.partial(compute, sizes, dims), out_shape=(jax.Sh...  1.34 us

profile of v4, /device:TPU:0, one launch (start us, length us, event | category | flops | bytes accessed | tf_op | source)
XLA Modules:
  0.0 10.4 jit_solution(11588435493893187911)
XLA Ops:
  0.6 8.4 %gather.1 = (bf16[8,2,128]{2,1,0:T(2,128)(2,1)S(1)}, bf16[9,32,256]{2,1,0:T(8,128)(2,1)S(1)}, bf16[2,128,384]{2,1,0:T(8,128)(2,1)S(1)}, f32[2,8,512]{2,1,0:T(8,128)S(1)}, f32[2,8,128]{2,1,0:T(8,128)S(1)}) custom-call(s32[2]{0:T(128)} %refs_0_.1, s32[2]{0:T(128)} %refs_1_.1, s32[2]{0:T(128)} %refs_2_.1, s32[2]{0:T(128)} %refs_3_.1, ...), custom_call_target="tpu_custom_call" | custom-call | tf_op jit(solution)/shard_map/gather/pallas_call | solution.py:467
  9.0 1.3 %compute.1 = (bf16[2,8,2,512]{3,2,1,0:T(2,128)(2,1)}, f32[2,8,512]{2,1,0:T(8,128)}) custom-call(bf16[8,2,128]{2,1,0:T(2,128)(2,1)S(1)} %get-tuple-element.7.taps_ref, bf16[9,32,256]{2,1,0:T(8,128)(2,1)S(1)} %get-tuple-element.8.xa, bf16[2,128,384]{2,1,0:T(8,128)(2,1)S(1)} %get-tuple-element.9.weights, f32[2,8,512]{2,1,0:T(8,128)S(1)} %get-tuple-element.10.counts, ...), custom_call_target="tpu_custom_call" | custom-call | tf_op jit(solution)/shard_map/compute/pallas_call | solution.py:500

commit v5 on v4

--- a/solution.py
+++ b/solution.py
@@ -129,22 +129,33 @@
         ]
 
     def same_plane():
-        return tap_copies(rep, me, 0, bi)
+        return tap_copies(rep, pi * planes + bi, 0, bi)
 
     def down(b, source):
-        return tap_copies(source, b * npulse + pi, 1 + b, bi - 1)
+        return tap_copies(source, pi * planes + b, 1 + b, bi - 1)
 
     def up(b, source):
-        return tap_copies(source, b * npulse + pi, 1 + planes + b, bi + 1)
-
-    def beyond(b, source, q):
-        way = 1 + (2 + q - planes) * planes + b
-        return tap_copies(source, b * npulse + pi, way, q)
-
-    def arrived(slot):
+        return tap_copies(source, pi * planes + b, 1 + planes + b, bi + 1)
+
+    def beyond(q):
+        column = hbuf.at[pl.ds(pi * planes, planes)]
+        return [
+            pltpu.make_async_remote_copy(
+                src_ref=column,
+                dst_ref=column,
+                send_sem=hsend.at[1 + planes + q, j],
+                recv_sem=hrecv.at[pi * planes],
+                device_id={"beam": q, "pulse": lax.rem(pi + j, npulse)},
+                device_id_type=MESH,
+            )
+            for j in range(npulse)
+        ]
+
+    def arrived(slot, count=1):
+        spot = hbuf.at[pl.ds(slot, count)]
         copy = pltpu.make_async_remote_copy(
-            src_ref=rep,
-            dst_ref=hbuf.at[slot],
+            src_ref=spot,
+            dst_ref=spot,
             send_sem=hsend.at[0, 0],
             recv_sem=hrecv.at[slot],
             device_id={"beam": bi},
@@ -171,10 +182,11 @@
             if b >= 1:
                 for copy in down(b, rep):
                     copy.start()
+            rest = same_plane()
             if b + 1 < planes:
-                for copy in up(b, rep):
-                    copy.start()
-            for copy in same_plane():
+                first, *others = up(b, rep)
+                rest = [first] + rest + others
+            for copy in rest:
                 copy.start()
 
     for s in range(1, reach + 1):
@@ -188,7 +200,7 @@
         tail_copy().start()
 
     def own_taps():
-        return pltpu.make_async_copy(rep, hbuf.at[me], here.at[5])
+        return pltpu.make_async_copy(rep, hbuf.at[pi * planes + bi], here.at[5])
 
     @pl.when(me < senders)
     def _():
@@ -232,7 +244,7 @@
 
         @pl.when((bi < planes) & (bi != b) & (bi >= 1))
         def _():
-            slot = b * npulse + pi
+            slot = pi * planes + b
             arrived(slot)
 
             @pl.when(bi < b)
@@ -247,12 +259,11 @@
 
     @pl.when(bi == planes - 1)
     def _():
+        own_taps().wait()
         for q in range(planes, nb):
             pl.semaphore_wait(ready.at[q - planes], npulse)
-            for b in range(planes):
-                source = rep if b == planes - 1 else hbuf.at[b * npulse + pi]
-                for copy in beyond(b, source, q):
-                    copy.start()
+            for copy in beyond(q):
+                copy.start()
 
     @pl.when(ri >= 1)
     def _():
@@ -303,17 +314,23 @@
         second = jnp.concatenate([imag, -real], axis=1)
         xa[c] = jnp.concatenate([first, second], axis=0).astype(jnp.bfloat16)
 
-    @pl.when(me < senders)
+    @pl.when(bi < planes - 1)
     def _():
         own_taps().wait()
 
     for slot in range(senders):
 
-        first = (bi == 0) & (slot >= npulse)
-
-        @pl.when((pi != slot % npulse) | (bi >= planes) | first)
+        late = (bi == 0) & (slot % planes > 0)
+
+        @pl.when((bi < planes) & ((pi != slot // planes) | late))
         def _():
             arrived(slot)
+
+    for j in range(npulse):
+
+        @pl.when(bi >= planes)
+        def _():
+            arrived(j * planes, planes)
 
     hout[...] = hbuf[...]
 
@@ -337,9 +354,8 @@
     @pl.when(bi == planes - 1)
     def _():
         for q in range(planes, nb):
-            for b in range(planes):
-                for copy in beyond(b, rep, q):
-                    copy.wait_send()
+            for copy in beyond(q):
+                copy.wait_send()
 
     for s in range(1, reach + 1):
 
@@ -363,12 +379,17 @@
     per = TILE // piece if piece < TILE else 1
     spread = max(piece // TILE, 1)
 
+    planes = senders // sizes[1]
+
+    def taps_at(s):
+        return taps_ref[(s % sizes[1]) * planes + s // sizes[1]].astype(jnp.float32)
+
     def taps_of(c):
         if piece >= TILE:
-            return taps_ref[c // spread].astype(jnp.float32)[
+            return taps_at(c // spread)[
                 :, (c % spread) * TILE : (c % spread + 1) * TILE
             ]
-        parts = [taps_ref[c * per + i].astype(jnp.float32) for i in range(per)]
+        parts = [taps_at(c * per + i) for i in range(per)]
         return jnp.concatenate(parts, axis=1)
 
     held = min(panels, (senders * piece) // TILE)
@@ -485,7 +506,7 @@
         + [pltpu.SMEM((beams,), jnp.int32)] * 4
         + [
             pltpu.SemaphoreType.DMA((6,)),
-            pltpu.SemaphoreType.DMA((1 + planes * (2 + sizes[0] - planes), sizes[1])),
+            pltpu.SemaphoreType.DMA((1 + 2 * planes + sizes[0], sizes[1])),
             pltpu.SemaphoreType.DMA((senders,)),
             pltpu.SemaphoreType.DMA((reach + 1,)),
             pltpu.SemaphoreType.DMA((reach + 1,)),

time: 10.5 us -> 10.5 us (level)
  no operation moved by 1% of the time
where the time goes in v5:
time: 10.5 us; the launch traced here: 10.4 us
  Pallas kernels  9.74 us (93%)
  between operations  0.64 us (6%)
    pallas_call x1, Pallas kernels, body(): pl.pallas_call(functools.partial(gather, sizes, dims), out_shape=(jax.Sha...  8.4 us
    pallas_call x1, Pallas kernels, body(): pl.pallas_call(functools.partial(compute, sizes, dims), out_shape=(jax.Sh...  1.34 us

profile of v5, /device:TPU:0, one launch (start us, length us, event | category | flops | bytes accessed | tf_op | source)
XLA Modules:
  0.0 10.4 jit_solution(662425418355548832)
XLA Ops:
  0.6 8.4 %gather.1 = (bf16[8,2,128]{2,1,0:T(2,128)(2,1)S(1)}, bf16[9,32,256]{2,1,0:T(8,128)(2,1)S(1)}, bf16[2,128,384]{2,1,0:T(8,128)(2,1)S(1)}, f32[2,8,512]{2,1,0:T(8,128)S(1)}, f32[2,8,128]{2,1,0:T(8,128)S(1)}) custom-call(s32[2]{0:T(128)} %refs_0_.1, s32[2]{0:T(128)} %refs_1_.1, s32[2]{0:T(128)} %refs_2_.1, s32[2]{0:T(128)} %refs_3_.1, ...), custom_call_target="tpu_custom_call" | custom-call | tf_op jit(solution)/shard_map/gather/pallas_call | solution.py:488
  9.0 1.3 %compute.1 = (bf16[2,8,2,512]{3,2,1,0:T(2,128)(2,1)}, f32[2,8,512]{2,1,0:T(8,128)}) custom-call(bf16[8,2,128]{2,1,0:T(2,128)(2,1)S(1)} %get-tuple-element.7.taps_ref, bf16[9,32,256]{2,1,0:T(8,128)(2,1)S(1)} %get-tuple-element.8.xa, bf16[2,128,384]{2,1,0:T(8,128)(2,1)S(1)} %get-tuple-element.9.weights, f32[2,8,512]{2,1,0:T(8,128)S(1)} %get-tuple-element.10.counts, ...), custom_call_target="tpu_custom_call" | custom-call | tf_op jit(solution)/shard_map/compute/pallas_call | solution.py:521

commit v6 on v5

--- a/solution.py
+++ b/solution.py
@@ -122,10 +122,10 @@
                 dst_ref=hbuf.at[slot],
                 send_sem=hsend.at[way, j],
                 recv_sem=hrecv.at[slot],
-                device_id={"beam": plane, "pulse": lax.rem(pi + j, npulse)},
+                device_id={"beam": plane, "pulse": j},
                 device_id_type=MESH,
             )
-            for j in range(1 if way == 0 else 0, npulse)
+            for j in range(npulse)
         ]
 
     def same_plane():
@@ -182,12 +182,11 @@
             if b >= 1:
                 for copy in down(b, rep):
                     copy.start()
-            rest = same_plane()
+            for j, copy in enumerate(same_plane()):
+                pl.when(pi != j)(copy.start)
             if b + 1 < planes:
-                first, *others = up(b, rep)
-                rest = [first] + rest + others
-            for copy in rest:
-                copy.start()
+                for copy in up(b, rep):
+                    copy.start()
 
     for s in range(1, reach + 1):
 
@@ -336,8 +335,8 @@
 
     @pl.when(bi < planes)
     def _():
-        for copy in same_plane():
-            copy.wait_send()
+        for j, copy in enumerate(same_plane()):
+            pl.when(pi != j)(copy.wait_send)
 
     for b in range(planes):
 

time: 10.5 us -> 10.5 us (level)
  no operation moved by 1% of the time
where the time goes in v6:
time: 10.5 us; the launch traced here: 10.4 us
  Pallas kernels  9.74 us (93%)
  between operations  0.64 us (6%)
    pallas_call x1, Pallas kernels, body(): pl.pallas_call(functools.partial(gather, sizes, dims), out_shape=(jax.Sha...  8.41 us
    pallas_call x1, Pallas kernels, body(): pl.pallas_call(functools.partial(compute, sizes, dims), out_shape=(jax.Sh...  1.34 us

profile of v6, /device:TPU:0, one launch (start us, length us, event | category | flops | bytes accessed | tf_op | source)
XLA Modules:
  0.0 10.4 jit_solution(4268216030175932982)
XLA Ops:
  0.6 8.4 %gather.1 = (bf16[8,2,128]{2,1,0:T(2,128)(2,1)S(1)}, bf16[9,32,256]{2,1,0:T(8,128)(2,1)S(1)}, bf16[2,128,384]{2,1,0:T(8,128)(2,1)S(1)}, f32[2,8,512]{2,1,0:T(8,128)S(1)}, f32[2,8,128]{2,1,0:T(8,128)S(1)}) custom-call(s32[2]{0:T(128)} %refs_0_.1, s32[2]{0:T(128)} %refs_1_.1, s32[2]{0:T(128)} %refs_2_.1, s32[2]{0:T(128)} %refs_3_.1, ...), custom_call_target="tpu_custom_call" | custom-call | tf_op jit(solution)/shard_map/gather/pallas_call | solution.py:487
  9.0 1.3 %compute.1 = (bf16[2,8,2,512]{3,2,1,0:T(2,128)(2,1)}, f32[2,8,512]{2,1,0:T(8,128)}) custom-call(bf16[8,2,128]{2,1,0:T(2,128)(2,1)S(1)} %get-tuple-element.7.taps_ref, bf16[9,32,256]{2,1,0:T(8,128)(2,1)S(1)} %get-tuple-element.8.xa, bf16[2,128,384]{2,1,0:T(8,128)(2,1)S(1)} %get-tuple-element.9.weights, f32[2,8,512]{2,1,0:T(8,128)S(1)} %get-tuple-element.10.counts, ...), custom_call_target="tpu_custom_call" | custom-call | tf_op jit(solution)/shard_map/compute/pallas_call | solution.py:520

commit v7 on v6

--- a/solution.py
+++ b/solution.py
@@ -62,12 +62,10 @@
         for j in range(1, npulse):
             say(barrier, bi, lax.rem(pi + j, npulse))
 
-    for side in (-1, 1):
-
-        @pl.when((bi < planes) & (bi + side >= 0) & (bi + side < planes))
-        def _():
-            for j in range(npulse):
-                say(barrier, bi + side, lax.rem(pi + j, npulse))
+    @pl.when(bi + 1 < planes)
+    def _():
+        for j in range(npulse):
+            say(barrier, bi + 1, lax.rem(pi + j, npulse))
 
     @pl.when(bi == planes - 1)
     def _():
@@ -164,9 +162,15 @@
         copy.wait_recv()
 
     expect = jnp.minimum(ri, reach) + jnp.where(ri + 1 < nr, 1, 0)
-    beside = jnp.where(bi >= 1, npulse, 0) + jnp.where(bi + 1 < planes, npulse, 0)
+    beside = jnp.where(bi >= 1, npulse, 0)
     expect += jnp.where(bi < planes, npulse - 1 + beside, npulse)
     pl.semaphore_wait(barrier, expect)
+    above = ready.at[nb - planes]
+
+    @pl.when((bi < planes) & (bi >= 1))
+    def _():
+        for j in range(npulse):
+            say(above, bi - 1, lax.rem(pi + j, npulse))
 
     for q in range(planes, nb):
 
@@ -184,9 +188,6 @@
                     copy.start()
             for j, copy in enumerate(same_plane()):
                 pl.when(pi != j)(copy.start)
-            if b + 1 < planes:
-                for copy in up(b, rep):
-                    copy.start()
 
     for s in range(1, reach + 1):
 
@@ -238,6 +239,16 @@
         counts[b] = count.astype(jnp.float32)
         level = jnp.full((pulses, TILE), scales[b], jnp.int32).astype(jnp.float32)
         factors[b] = jnp.exp2(level / 8.0)
+
+    @pl.when(bi + 1 < planes)
+    def _():
+        pl.semaphore_wait(above, npulse)
+        for b in range(planes - 1):
+
+            @pl.when(bi == b)
+            def _():
+                for copy in up(b, rep):
+                    copy.start()
 
     for b in reversed(range(planes)):
 
@@ -509,7 +520,7 @@
             pltpu.SemaphoreType.DMA((senders,)),
             pltpu.SemaphoreType.DMA((reach + 1,)),
             pltpu.SemaphoreType.DMA((reach + 1,)),
-            pltpu.SemaphoreType.REGULAR((max(sizes[0] - planes, 1),)),
+            pltpu.SemaphoreType.REGULAR((sizes[0] - planes + 1,)),
         ]
         + [pltpu.VMEM((beams, pulses, 2, keep), jnp.bfloat16) for keep in keeps],
         compiler_params=pltpu.CompilerParams(

time: 10.5 us -> 11.3 us (1.076)
  the two profiles are of different devices: /device:TPU:0 before, /device:TPU:17 now
where the time goes in v7:
time: 11.3 us; the launch traced here: 11.2 us
  Pallas kernels  10.5 us (93%)
  between operations  0.64 us (6%)
    pallas_call x1, Pallas kernels, body(): pl.pallas_call(functools.partial(gather, sizes, dims), out_shape=(jax.Sha...  9.2 us
    pallas_call x1, Pallas kernels, body(): pl.pallas_call(functools.partial(compute, sizes, dims), out_shape=(jax.Sh...  1.34 us

profile of v7, /device:TPU:17, one launch (start us, length us, event | category | flops | bytes accessed | tf_op | source)
XLA Modules:
  0.0 11.2 jit_solution(8794102664191470093)
XLA Ops:
  0.6 9.2 %gather.1 = (bf16[8,2,128]{2,1,0:T(2,128)(2,1)S(1)}, bf16[9,32,256]{2,1,0:T(8,128)(2,1)S(1)}, bf16[2,128,384]{2,1,0:T(8,128)(2,1)S(1)}, f32[2,8,512]{2,1,0:T(8,128)S(1)}, f32[2,8,128]{2,1,0:T(8,128)S(1)}) custom-call(s32[2]{0:T(128)} %refs_0_.1, s32[2]{0:T(128)} %refs_1_.1, s32[2]{0:T(128)} %refs_2_.1, s32[2]{0:T(128)} %refs_3_.1, ...), custom_call_target="tpu_custom_call" | custom-call | tf_op jit(solution)/shard_map/gather/pallas_call | solution.py:498
  9.8 1.3 %compute.1 = (bf16[2,8,2,512]{3,2,1,0:T(2,128)(2,1)}, f32[2,8,512]{2,1,0:T(8,128)}) custom-call(bf16[8,2,128]{2,1,0:T(2,128)(2,1)S(1)} %get-tuple-element.7.taps_ref, bf16[9,32,256]{2,1,0:T(8,128)(2,1)S(1)} %get-tuple-element.8.xa, bf16[2,128,384]{2,1,0:T(8,128)(2,1)S(1)} %get-tuple-element.9.weights, f32[2,8,512]{2,1,0:T(8,128)S(1)} %get-tuple-element.10.counts, ...), custom_call_target="tpu_custom_call" | custom-call | tf_op jit(solution)/shard_map/compute/pallas_call | solution.py:531
